TPU v7x, 256 devices: a whole 4x4x8 slice. The times are simulated.
256 devices in a mesh: layer: 8 (over y, core), trace: 32 (over x, z).
Axes of the slice: x: 4, y: 4, z: 8, core: 2. Of those that a mesh axis runs over, the one named last changes fastest.
Arguments:
- source_up: bfloat16 [8, 32768, 256], P('layer', 'trace'), may hold values from -6 to 6
- source_down: bfloat16 [8, 32768, 256], P('layer', 'trace'), may hold values from -6 to 6
- diag_up: bfloat16 [8, 2, 32768, 1024], P('layer', None, 'trace'), may hold values from -0.125 to 0.125
- diag_down: bfloat16 [8, 2, 32768, 1024], P('layer', None, 'trace'), may hold values from -0.125 to 0.125
- projection: bfloat16 [8, 2, 32, 32768], P('layer', None, None, 'trace'), may hold values from -0.1875 to 0.1875
- expansion: bfloat16 [8, 2, 32, 32768], P('layer', None, None, 'trace'), may hold values from -1 to 1
- coupling: bfloat16 [8, 2, 2, 1024, 1024], P('layer', None, None, 'trace'), may hold values from -0.125 to 0.125
Outputs:
- trace_up: bfloat16 [8, 32768, 256], P('layer', 'trace')
- trace_down: bfloat16 [8, 32768, 256], P('layer', 'trace')
All inputs are finite; a program needn't handle non-finite values.
Results may differ from a plain program's by a relative error of at most 0.013.
Values may be sent and summed in bfloat16 or wider, within the bound.
A program may use at most 64 MiB of HBM per device.

v0:
```python
import jax
import jax.numpy as jnp
from jax import lax
from jax.sharding import PartitionSpec as P

ITERS = 3


def for_sending(shard):

    def short(part):
        return part.astype(jnp.bfloat16) if part.dtype == jnp.float32 else part

    return jax.tree.map(short, shard)


def copy_for_each(shard, axis):
    copies = jnp.broadcast_to(shard, (lax.axis_size(axis), *shard.shape))
    return lax.all_to_all(copies, axis, split_axis=0, concat_axis=0, tiled=True)


def laid_out(pieces, dim):
    pieces = jnp.moveaxis(pieces, 0, dim)
    shape = pieces.shape
    return pieces.reshape(*shape[:dim], shape[dim] * shape[dim + 1], *shape[dim + 2 :])


def gather_directly(shard, axis, dim):
    pieces = copy_for_each(shard, axis)
    return laid_out(pieces, dim)


def shifted(value, axis, steps):
    count = lax.axis_size(axis)
    initial, last = (max(0, -steps), min(count, count - steps))
    return lax.ppermute(value, axis, [(source, source + steps) for source in range(initial, last)])


def rotate(field):
    half = field.shape[-1] // 2
    return jnp.concatenate([-field[..., half:], field[..., :half]], axis=-1)


def shards(source_up, source_down, diag_up, diag_down, projection, expansion, coupling):
    upward = source_up[0]
    downward = source_down[0]
    blocks = (diag_up[0], diag_down[0])
    for step in range(ITERS):
        fields = (upward, downward)
        coeffs = tuple(
            (
                jnp.dot(
                    projection[0, which], fields[which], preferred_element_type=jnp.float32
                ).astype(jnp.bfloat16)
                for which in range(2)
            )
        )
        gathered = jax.tree.map(
            lambda part, own: part.astype(own.dtype),
            jax.tree.map(lambda part: gather_directly(part, "trace", 0), for_sending(coeffs)),
            coeffs,
        )
        coupled = tuple(
            (
                (
                    jnp.dot(
                        coupling[0, which, 0], gathered[which], preferred_element_type=jnp.float32
                    )
                    + jnp.dot(
                        coupling[0, which, 1],
                        rotate(gathered[which]),
                        preferred_element_type=jnp.float32,
                    )
                ).astype(jnp.bfloat16)
                for which in range(2)
            )
        )
        results = []
        for which in range(2):
            block = blocks[which]
            result = jnp.dot(block[0], fields[which], preferred_element_type=jnp.float32)
            result = result + jnp.dot(
                block[1], rotate(fields[which]), preferred_element_type=jnp.float32
            )
            result = result + lax.dot_general(
                expansion[0, which],
                coupled[which],
                (((0,), (0,)), ((), ())),
                preferred_element_type=jnp.float32,
            )
            results.append(result.astype(jnp.bfloat16))
        arrived_up = shifted(results[0], "layer", 1)
        arrived_down = shifted(results[1], "layer", -1)
        upward = (source_up[0].astype(jnp.float32) + arrived_up.astype(jnp.float32)).astype(
            jnp.bfloat16
        )
        downward = (source_down[0].astype(jnp.float32) + arrived_down.astype(jnp.float32)).astype(
            jnp.bfloat16
        )
    return (upward[None], downward[None])


def solution(mesh):
    return jax.shard_map(
        shards,
        mesh=mesh,
        in_specs=(
            P("layer", "trace", None),
            P("layer", "trace", None),
            P("layer", None, "trace", None),
            P("layer", None, "trace", None),
            P("layer", None, None, "trace"),
            P("layer", None, None, "trace"),
            P("layer", None, None, "trace", None),
        ),
        out_specs=(P("layer", "trace", None), P("layer", "trace", None)),
        check_vma=False,
    )
```

profile of v0, /device:TPU:9, one launch (start us, length us, event | category | flops | bytes accessed | tf_op | source)
XLA Modules:
  0.0 197.5 jit_solution(1592513696675533439)
XLA Ops:
  0.7 1.4 convolution_convert_fusion.5
  2.0 0.9 broadcast_in_dim.24
  2.9 11.0 %all-to-all-start = ((bf16[32,32,256]{2,1,0:T(8,128)(2,1)}), bf16[32,32,256]{2,1,0:T(8,128)(2,1)S(1)}, u32[]{:S(2)}, u32[]{:S(2)}) async-start(bf16[32,32,256]{2,1,0:T(8,128)(2,1)} %broadcast_in_dim.24), calls=%async_computation | async-start | bytes 1048576 | tf_op jit(solution)/shard_map/all_to_all | solution.py:19
  13.9 1.1 slice_negate_fusion.11
  15.0 1.1 slice_negate_fusion.5
  16.3 2.5 %fusion.22 = f32[1024,256]{1,0:T(8,128)S(1)} fusion(bf16[1,2,1024,1024]{3,2,1,0:T(8,128)(2,1)} %param.9, bf16[1,1024,256]{2,1,0:T(8,128)(2,1)S(1)} %copy-done), kind=kOutput, calls=%fused_computation.22 | convolution fusion | flops 536870912 | bytes 3670016 | tf_op jit(solution)/shard_map/dot_general | solution.py:81
  18.9 1.7 fusion.10
  20.6 0.9 copy-done.2
  21.5 1.7 fusion.47
  23.2 5.2 %all-to-all-done = bf16[32,32,256]{2,1,0:T(8,128)(2,1)S(1)} async-done(((bf16[32,32,256]{2,1,0:T(8,128)(2,1)}), bf16[32,32,256]{2,1,0:T(8,128)(2,1)S(1)}, u32[]{:S(2)}, u32[]{:S(2)}) %all-to-all-start) | async-done | bytes 524320 | tf_op jit(solution)/shard_map/all_to_all | solution.py:19
  28.5 0.9 broadcast_in_dim.28
  29.3 7.3 %all-to-all-start.3 = ((bf16[32,32,256]{2,1,0:T(8,128)(2,1)}), bf16[32,32,256]{2,1,0:T(8,128)(2,1)S(1)}, u32[]{:S(2)}, u32[]{:S(2)}) async-start(bf16[32,32,256]{2,1,0:T(8,128)(2,1)} %broadcast_in_dim.28), calls=%async_computation.3 | async-start | bytes 1048576 | tf_op jit(solution)/shard_map/all_to_all | solution.py:19
  36.6 3.5 %fusion.44 = f32[1024,256]{1,0:T(8,128)} fusion(f32[1024,256]{1,0:T(8,128)} %fusion.10, bf16[1,2,1024,1024]{3,2,1,0:T(8,128)(2,1)} %param.10, bf16[1024,128]{1,0:T(8,128)(2,1)S(1)} %get-tuple-element.13, bf16[1024,128]{1,0:T(8,128)(2,1)S(1)} %get-tuple-element.12), kind=kOutput, calls=%fused_computation.48 | convolution fusion | flops 538181632 | bytes 4718592 | tf_op jit(solution)/shard_map/dot_general | solution.py:82
  40.1 0.3 fusion.207
  40.5 2.6 %fusion.86 = bf16[1024,256]{1,0:T(8,128)(2,1)} fusion(f32[1024,256]{1,0:T(8,128)} %fusion.47, f32[256,32]{1,0:T(8,128)S(1)} %fusion.207, bf16[1024,128]{1,0:T(8,128)(2,1)S(1)} %get-tuple-element.23, bf16[1024,128]{1,0:T(8,128)(2,1)S(1)} %get-tuple-element.22, bf16[1,2,32,1024]{3,2,1,0:T(8,128)(2,1)S(1)} %copy-done.6, ...), kind=kOutput, calls=%fused_computation.62 | convolution fusion | flops 35143680 | bytes 2359296 | tf_op jit(solution)/shard_map/dot_general | solution.py:85
  43.2 4.7 %collective-permute-start = (bf16[1024,256]{1,0:T(8,128)(2,1)}, bf16[1024,256]{1,0:T(8,128)(2,1)S(1)}, u32[]{:S(2)}, u32[]{:S(2)}) collective-permute-start(bf16[1024,256]{1,0:T(8,128)(2,1)} %fusion.86), channel_id=1, source_target_pairs={{0,32},{32,64},{64,96},{96,128},{128,160},{160,192},{192,224},{1,3... | collective-permute-start | bytes 1572872 | tf_op jit(solution)/shard_map/ppermute | solution.py:36
  47.9 2.5 %all-to-all-done.3 = bf16[32,32,256]{2,1,0:T(8,128)(2,1)S(1)} async-done(((bf16[32,32,256]{2,1,0:T(8,128)(2,1)}), bf16[32,32,256]{2,1,0:T(8,128)(2,1)S(1)}, u32[]{:S(2)}, u32[]{:S(2)}) %all-to-all-start.3) | async-done | bytes 524320 | tf_op jit(solution)/shard_map/all_to_all | solution.py:19
  50.4 0.3 fusion.189
  50.8 1.8 fusion.87
  52.6 6.3 %collective-permute-start.3 = (bf16[1024,256]{1,0:T(8,128)(2,1)S(1)}, bf16[1024,256]{1,0:T(8,128)(2,1)}, u32[]{:S(2)}, u32[]{:S(2)}) collective-permute-start(bf16[1024,256]{1,0:T(8,128)(2,1)S(1)} %fusion.87), channel_id=1, source_target_pairs={{32,0},{64,32},{96,64},{128,96},{160,128},{192,160},{224,192},{33,... | collective-permute-start | bytes 1572872 | tf_op jit(solution)/shard_map/ppermute | solution.py:36
  59.2 0.9 broadcast_in_dim.25
  60.1 5.0 %all-to-all-start.1 = ((bf16[32,32,256]{2,1,0:T(8,128)(2,1)}), bf16[32,32,256]{2,1,0:T(8,128)(2,1)S(1)}, u32[]{:S(2)}, u32[]{:S(2)}) async-start(bf16[32,32,256]{2,1,0:T(8,128)(2,1)} %broadcast_in_dim.25), calls=%async_computation.1 | async-start | bytes 1048576 | tf_op jit(solution)/shard_map/all_to_all | solution.py:19
  65.1 1.9 collective-permute-done.3
  67.0 1.2 fusion.117
  68.5 3.3 %fusion.14 = f32[256,1024]{0,1:T(8,128)} fusion(bf16[1,2,1024,1024]{3,2,1,0:T(8,128)(2,1)} %param.9, bf16[1024,128]{1,0:T(8,128)(2,1)S(1)} %get-tuple-element.19, bf16[1024,128]{1,0:T(8,128)(2,1)S(1)} %get-tuple-element.18), kind=kOutput, calls=%fused_computation.14 | convolution fusion | flops 537919488 | bytes 3670016 | tf_op jit(solution)/shard_map/dot_general | solution.py:82
  71.8 7.4 %all-to-all-done.1 = bf16[32,32,256]{2,1,0:T(8,128)(2,1)S(1)} async-done(((bf16[32,32,256]{2,1,0:T(8,128)(2,1)}), bf16[32,32,256]{2,1,0:T(8,128)(2,1)S(1)}, u32[]{:S(2)}, u32[]{:S(2)}) %all-to-all-start.1) | async-done | bytes 524320 | tf_op jit(solution)/shard_map/all_to_all | solution.py:19
  79.1 0.9 broadcast_in_dim.29
  80.0 7.8 %all-to-all-start.4 = ((bf16[32,32,256]{2,1,0:T(8,128)(2,1)}), bf16[32,32,256]{2,1,0:T(8,128)(2,1)S(1)}, u32[]{:S(2)}, u32[]{:S(2)}) async-start(bf16[32,32,256]{2,1,0:T(8,128)(2,1)} %broadcast_in_dim.29), calls=%async_computation.4 | async-start | bytes 1048576 | tf_op jit(solution)/shard_map/all_to_all | solution.py:19
  87.9 3.3 %fusion.2 = f32[256,1024]{0,1:T(8,128)} fusion(bf16[1,2,1024,1024]{3,2,1,0:T(8,128)(2,1)} %param.10, bf16[1024,128]{1,0:T(8,128)(2,1)S(1)} %get-tuple-element.7, bf16[1024,128]{1,0:T(8,128)(2,1)S(1)} %get-tuple-element.6), kind=kOutput, calls=%fused_computation.2 | convolution fusion | flops 537919488 | bytes 3670016 | tf_op jit(solution)/shard_map/dot_general | solution.py:82
  91.2 1.0 fusion.205
  92.2 0.9 slice_negate_fusion.8
  93.0 8.7 %all-to-all-done.4 = bf16[32,32,256]{2,1,0:T(8,128)(2,1)S(1)} async-done(((bf16[32,32,256]{2,1,0:T(8,128)(2,1)}), bf16[32,32,256]{2,1,0:T(8,128)(2,1)S(1)}, u32[]{:S(2)}, u32[]{:S(2)}) %all-to-all-start.4) | async-done | bytes 524320 | tf_op jit(solution)/shard_map/all_to_all | solution.py:19
  101.8 1.0 fusion.187
  102.7 0.9 slice_negate_fusion.2
  103.6 1.7 fusion.109
  105.3 3.4 %fusion.91 = bf16[1024,256]{1,0:T(8,128)(2,1)} fusion(f32[256,1024]{0,1:T(8,128)S(1)} %fusion.109, f32[256,1024]{0,1:T(8,128)} %fusion.14, bf16[1024,256]{1,0:T(8,128)(2,1)S(1)} %fusion.114, bf16[1,2,1024,1024]{3,2,1,0:T(8,128)(2,1)} %param.9), kind=kOutput, calls=%fused_computation.65 | convolution fusion | flops 537657344 | bytes 5242880 | tf_op jit(solution)/shard_map/dot_general | solution.py:81
  108.7 7.3 %collective-permute-start.1 = (bf16[1024,256]{1,0:T(8,128)(2,1)}, bf16[1024,256]{1,0:T(8,128)(2,1)}, u32[]{:S(2)}, u32[]{:S(2)}) collective-permute-start(bf16[1024,256]{1,0:T(8,128)(2,1)} %fusion.91), channel_id=1, source_target_pairs={{0,32},{32,64},{64,96},{96,128},{128,160},{160,192},{192,224},{1,3... | collective-permute-start | bytes 1572872 | tf_op jit(solution)/shard_map/ppermute | solution.py:36
  115.9 1.7 fusion.107
  117.6 3.4 %fusion.97 = bf16[1024,256]{1,0:T(8,128)(2,1)} fusion(f32[256,1024]{0,1:T(8,128)S(1)} %fusion.107, f32[256,1024]{0,1:T(8,128)} %fusion.2, bf16[1024,256]{1,0:T(8,128)(2,1)S(1)} %fusion.117, bf16[1,2,1024,1024]{3,2,1,0:T(8,128)(2,1)} %param.10), kind=kOutput, calls=%fused_computation.67 | convolution fusion | flops 537657344 | bytes 5242880 | tf_op jit(solution)/shard_map/dot_general | solution.py:81
  121.0 1.9 collective-permute-start.4
  122.9 1.2 fusion.115
  124.3 0.9 broadcast_in_dim.26
  125.2 5.2 %all-to-all-start.2 = ((bf16[32,32,256]{2,1,0:T(8,128)(2,1)}), bf16[32,32,256]{2,1,0:T(8,128)(2,1)S(1)}, u32[]{:S(2)}, u32[]{:S(2)}) async-start(bf16[32,32,256]{2,1,0:T(8,128)(2,1)} %broadcast_in_dim.26), calls=%async_computation.2 | async-start | bytes 1048576 | tf_op jit(solution)/shard_map/all_to_all | solution.py:19
  130.3 1.3 collective-permute-done.4
  132.1 3.3 %fusion.16 = f32[256,1024]{0,1:T(8,128)} fusion(bf16[1,2,1024,1024]{3,2,1,0:T(8,128)(2,1)} %param.9, bf16[1024,128]{1,0:T(8,128)(2,1)S(1)} %get-tuple-element.15, bf16[1024,128]{1,0:T(8,128)(2,1)S(1)} %get-tuple-element.14), kind=kOutput, calls=%fused_computation.16 | convolution fusion | flops 537919488 | bytes 3670016 | tf_op jit(solution)/shard_map/dot_general | solution.py:82
  135.4 9.5 %all-to-all-done.2 = bf16[32,32,256]{2,1,0:T(8,128)(2,1)S(1)} async-done(((bf16[32,32,256]{2,1,0:T(8,128)(2,1)}), bf16[32,32,256]{2,1,0:T(8,128)(2,1)S(1)}, u32[]{:S(2)}, u32[]{:S(2)}) %all-to-all-start.2) | async-done | bytes 524320 | tf_op jit(solution)/shard_map/all_to_all | solution.py:19
  144.8 0.9 broadcast_in_dim.30
  145.7 7.1 %all-to-all-start.5 = ((bf16[32,32,256]{2,1,0:T(8,128)(2,1)}), bf16[32,32,256]{2,1,0:T(8,128)(2,1)S(1)}, u32[]{:S(2)}, u32[]{:S(2)}) async-start(bf16[32,32,256]{2,1,0:T(8,128)(2,1)} %broadcast_in_dim.30), calls=%async_computation.5 | async-start | bytes 1048576 | tf_op jit(solution)/shard_map/all_to_all | solution.py:19
  152.9 3.3 %fusion.4 = f32[256,1024]{0,1:T(8,128)} fusion(bf16[1,2,1024,1024]{3,2,1,0:T(8,128)(2,1)} %param.10, bf16[1024,128]{1,0:T(8,128)(2,1)S(1)} %get-tuple-element.3, bf16[1024,128]{1,0:T(8,128)(2,1)S(1)} %get-tuple-element.2), kind=kOutput, calls=%fused_computation.4 | convolution fusion | flops 537919488 | bytes 3670016 | tf_op jit(solution)/shard_map/dot_general | solution.py:82
  156.2 1.0 fusion.203
  157.2 0.9 slice_negate_fusion.6
  158.1 8.6 %all-to-all-done.5 = bf16[32,32,256]{2,1,0:T(8,128)(2,1)S(1)} async-done(((bf16[32,32,256]{2,1,0:T(8,128)(2,1)}), bf16[32,32,256]{2,1,0:T(8,128)(2,1)S(1)}, u32[]{:S(2)}, u32[]{:S(2)}) %all-to-all-start.5) | async-done | bytes 524320 | tf_op jit(solution)/shard_map/all_to_all | solution.py:19
  166.7 1.0 fusion.185
  167.7 0.9 slice_negate_fusion
  168.5 1.7 fusion.108
  170.2 3.4 %fusion.88 = bf16[1024,256]{1,0:T(8,128)(2,1)} fusion(f32[256,1024]{0,1:T(8,128)S(1)} %fusion.108, f32[256,1024]{0,1:T(8,128)} %fusion.16, bf16[1024,256]{1,0:T(8,128)(2,1)S(1)} %fusion.115, bf16[1,2,1024,1024]{3,2,1,0:T(8,128)(2,1)} %param.9), kind=kOutput, calls=%fused_computation.64 | convolution fusion | flops 537657344 | bytes 5242880 | tf_op jit(solution)/shard_map/dot_general | solution.py:81
  173.6 8.3 %collective-permute-start.2 = (bf16[1024,256]{1,0:T(8,128)(2,1)}, bf16[1024,256]{1,0:T(8,128)(2,1)S(1)}, u32[]{:S(2)}, u32[]{:S(2)}) collective-permute-start(bf16[1024,256]{1,0:T(8,128)(2,1)} %fusion.88), channel_id=1, source_target_pairs={{0,32},{32,64},{64,96},{96,128},{128,160},{160,192},{192,224},{1,3... | collective-permute-start | bytes 1572872 | tf_op jit(solution)/shard_map/ppermute | solution.py:36
  181.9 1.7 fusion.106
  183.5 2.6 %fusion.94 = bf16[1024,256]{1,0:T(8,128)(2,1)S(1)} fusion(f32[256,1024]{0,1:T(8,128)S(1)} %fusion.106, f32[256,1024]{0,1:T(8,128)} %fusion.4, bf16[1024,256]{1,0:T(8,128)(2,1)S(1)} %fusion.118, bf16[1,2,1024,1024]{3,2,1,0:T(8,128)(2,1)} %param.10), kind=kOutput, calls=%fused_computation.66 | convolution fusion | flops 537657344 | bytes 5242880 | tf_op jit(solution)/shard_map/dot_general | solution.py:81
  186.1 1.9 collective-permute-start.5
  188.0 0.2 collective-permute-done.2
  188.3 0.9 fusion.121
  189.2 7.4 %collective-permute-done.5 = bf16[1024,256]{1,0:T(8,128)(2,1)S(1)} collective-permute-done((bf16[1024,256]{1,0:T(8,128)(2,1)S(1)}, bf16[1024,256]{1,0:T(8,128)(2,1)S(1)}, u32[]{:S(2)}, u32[]{:S(2)}) %collective-permute-start.5) | collective-permute-done | bytes 524320 | tf_op jit(solution)/shard_map/ppermute | solution.py:36
  196.6 0.9 fusion.120
  (30 shorter events, 1.8 us)
Async XLA Ops:
  0.6 15.7 %copy-start = (bf16[1,1024,256]{2,1,0:T(8,128)(2,1)S(1)}, bf16[1,1024,256]{2,1,0:T(8,128)(2,1)}, u32[]{:S(2)}) copy-start(bf16[1,1024,256]{2,1,0:T(8,128)(2,1)} %param.7) | copy-start | bytes 1572868
  0.6 15.5 %copy-start.5 = (bf16[1,2,32,1024]{3,2,1,0:T(8,128)(2,1)S(1)}, bf16[1,2,32,1024]{3,2,1,0:T(8,128)(2,1)}, u32[]{:S(2)}) copy-start(bf16[1,2,32,1024]{3,2,1,0:T(8,128)(2,1)} %param.11) | copy-start | bytes 393220
  0.7 15.5 %copy-start.1 = (bf16[1,1024,256]{2,1,0:T(8,128)(2,1)S(1)}, bf16[1,1024,256]{2,1,0:T(8,128)(2,1)}, u32[]{:S(2)}) copy-start(bf16[1,1024,256]{2,1,0:T(8,128)(2,1)} %param.8) | copy-start | bytes 1572868
  2.9 25.6 %all-to-all-start = ((bf16[32,32,256]{2,1,0:T(8,128)(2,1)}), bf16[32,32,256]{2,1,0:T(8,128)(2,1)S(1)}, u32[]{:S(2)}, u32[]{:S(2)}) async-start(bf16[32,32,256]{2,1,0:T(8,128)(2,1)} %broadcast_in_dim.24), calls=%async_computation | async-start | bytes 1048576 | tf_op jit(solution)/shard_map/all_to_all | solution.py:19
  16.1 2.8 %copy-start.3 = (bf16[1,2,1024,1024]{3,2,1,0:T(8,128)(2,1)S(1)}, bf16[1,2,1024,1024]{3,2,1,0:T(8,128)(2,1)}, u32[]{:S(2)}) copy-start(bf16[1,2,1024,1024]{3,2,1,0:T(8,128)(2,1)} %param.10) | copy-start | bytes 12582916
  18.9 2.6 %copy-start.2 = (bf16[1,2,1024,1024]{3,2,1,0:T(8,128)(2,1)S(1)}, bf16[1,2,1024,1024]{3,2,1,0:T(8,128)(2,1)}, u32[]{:S(2)}) copy-start(bf16[1,2,1024,1024]{3,2,1,0:T(8,128)(2,1)} %param.9) | copy-start | bytes 12582916
  23.2 16.9 %copy-start.4 = (bf16[1,2,2,32,1024]{4,3,2,1,0:T(8,128)(2,1)S(1)}, bf16[1,2,2,32,1024]{4,3,2,1,0:T(8,128)(2,1)}, u32[]{:S(2)}) copy-start(bf16[1,2,2,32,1024]{4,3,2,1,0:T(8,128)(2,1)} %param.13) | copy-start | bytes 786436
  23.2 17.3 %copy-start.6 = (bf16[1,2,32,1024]{3,2,1,0:T(8,128)(2,1)S(1)}, bf16[1,2,32,1024]{3,2,1,0:T(8,128)(2,1)}, u32[]{:S(2)}) copy-start(bf16[1,2,32,1024]{3,2,1,0:T(8,128)(2,1)} %param.12) | copy-start | bytes 393220
  29.3 21.1 %all-to-all-start.3 = ((bf16[32,32,256]{2,1,0:T(8,128)(2,1)}), bf16[32,32,256]{2,1,0:T(8,128)(2,1)S(1)}, u32[]{:S(2)}, u32[]{:S(2)}) async-start(bf16[32,32,256]{2,1,0:T(8,128)(2,1)} %broadcast_in_dim.28), calls=%async_computation.3 | async-start | bytes 1048576 | tf_op jit(solution)/shard_map/all_to_all | solution.py:19
  43.2 15.7 %collective-permute-start = (bf16[1024,256]{1,0:T(8,128)(2,1)}, bf16[1024,256]{1,0:T(8,128)(2,1)S(1)}, u32[]{:S(2)}, u32[]{:S(2)}) collective-permute-start(bf16[1024,256]{1,0:T(8,128)(2,1)} %fusion.86), channel_id=1, source_target_pairs={{0,32},{32,64},{64,96},{96,128},{128,160},{160,192},{192,224},{1,3... | collective-permute-start | bytes 1572872 | tf_op jit(solution)/shard_map/ppermute | solution.py:36
  52.6 14.4 %collective-permute-start.3 = (bf16[1024,256]{1,0:T(8,128)(2,1)S(1)}, bf16[1024,256]{1,0:T(8,128)(2,1)}, u32[]{:S(2)}, u32[]{:S(2)}) collective-permute-start(bf16[1024,256]{1,0:T(8,128)(2,1)S(1)} %fusion.87), channel_id=1, source_target_pairs={{32,0},{64,32},{96,64},{128,96},{160,128},{192,160},{224,192},{33,... | collective-permute-start | bytes 1572872 | tf_op jit(solution)/shard_map/ppermute | solution.py:36
  60.1 19.0 %all-to-all-start.1 = ((bf16[32,32,256]{2,1,0:T(8,128)(2,1)}), bf16[32,32,256]{2,1,0:T(8,128)(2,1)S(1)}, u32[]{:S(2)}, u32[]{:S(2)}) async-start(bf16[32,32,256]{2,1,0:T(8,128)(2,1)} %broadcast_in_dim.25), calls=%async_computation.1 | async-start | bytes 1048576 | tf_op jit(solution)/shard_map/all_to_all | solution.py:19
  80.0 21.8 %all-to-all-start.4 = ((bf16[32,32,256]{2,1,0:T(8,128)(2,1)}), bf16[32,32,256]{2,1,0:T(8,128)(2,1)S(1)}, u32[]{:S(2)}, u32[]{:S(2)}) async-start(bf16[32,32,256]{2,1,0:T(8,128)(2,1)} %broadcast_in_dim.29), calls=%async_computation.4 | async-start | bytes 1048576 | tf_op jit(solution)/shard_map/all_to_all | solution.py:19
  108.7 14.3 %collective-permute-start.1 = (bf16[1024,256]{1,0:T(8,128)(2,1)}, bf16[1024,256]{1,0:T(8,128)(2,1)}, u32[]{:S(2)}, u32[]{:S(2)}) collective-permute-start(bf16[1024,256]{1,0:T(8,128)(2,1)} %fusion.91), channel_id=1, source_target_pairs={{0,32},{32,64},{64,96},{96,128},{128,160},{160,192},{192,224},{1,3... | collective-permute-start | bytes 1572872 | tf_op jit(solution)/shard_map/ppermute | solution.py:36
  121.0 10.7 %collective-permute-start.4 = (bf16[1024,256]{1,0:T(8,128)(2,1)}, bf16[1024,256]{1,0:T(8,128)(2,1)S(1)}, u32[]{:S(2)}, u32[]{:S(2)}) collective-permute-start(bf16[1024,256]{1,0:T(8,128)(2,1)} %fusion.97), channel_id=1, source_target_pairs={{32,0},{64,32},{96,64},{128,96},{160,128},{192,160},{224,192},{33,... | collective-permute-start | bytes 1572872 | tf_op jit(solution)/shard_map/ppermute | solution.py:36
  125.2 19.7 %all-to-all-start.2 = ((bf16[32,32,256]{2,1,0:T(8,128)(2,1)}), bf16[32,32,256]{2,1,0:T(8,128)(2,1)S(1)}, u32[]{:S(2)}, u32[]{:S(2)}) async-start(bf16[32,32,256]{2,1,0:T(8,128)(2,1)} %broadcast_in_dim.26), calls=%async_computation.2 | async-start | bytes 1048576 | tf_op jit(solution)/shard_map/all_to_all | solution.py:19
  145.7 21.0 %all-to-all-start.5 = ((bf16[32,32,256]{2,1,0:T(8,128)(2,1)}), bf16[32,32,256]{2,1,0:T(8,128)(2,1)S(1)}, u32[]{:S(2)}, u32[]{:S(2)}) async-start(bf16[32,32,256]{2,1,0:T(8,128)(2,1)} %broadcast_in_dim.30), calls=%async_computation.5 | async-start | bytes 1048576 | tf_op jit(solution)/shard_map/all_to_all | solution.py:19
  152.9 15.6 %copy-start.7 = (bf16[1,2,32,1024]{3,2,1,0:T(8,128)(2,1)S(1)}, bf16[1,2,32,1024]{3,2,1,0:T(8,128)(2,1)}, u32[]{:S(2)}) copy-start(bf16[1,2,32,1024]{3,2,1,0:T(8,128)(2,1)} %param.12) | copy-start | bytes 393220
  173.6 14.7 %collective-permute-start.2 = (bf16[1024,256]{1,0:T(8,128)(2,1)}, bf16[1024,256]{1,0:T(8,128)(2,1)S(1)}, u32[]{:S(2)}, u32[]{:S(2)}) collective-permute-start(bf16[1024,256]{1,0:T(8,128)(2,1)} %fusion.88), channel_id=1, source_target_pairs={{0,32},{32,64},{64,96},{96,128},{128,160},{160,192},{192,224},{1,3... | collective-permute-start | bytes 1572872 | tf_op jit(solution)/shard_map/ppermute | solution.py:36
  186.1 10.5 %collective-permute-start.5 = (bf16[1024,256]{1,0:T(8,128)(2,1)S(1)}, bf16[1024,256]{1,0:T(8,128)(2,1)S(1)}, u32[]{:S(2)}, u32[]{:S(2)}) collective-permute-start(bf16[1024,256]{1,0:T(8,128)(2,1)S(1)} %fusion.94), channel_id=1, source_target_pairs={{32,0},{64,32},{96,64},{128,96},{160,128},{192,160},{224,192},{33,... | collective-permute-start | bytes 1572872 | tf_op jit(solution)/shard_map/ppermute | solution.py:36
where the time goes:
time: 200 us; the launch traced here: 198 us
  starting transfers between devices  73.9 us (37%)
  matrix products  53.3 us (27%)
  waiting for transfers between devices  52.8 us (26%)
  other arithmetic  10.5 us (5%)
  local copies, waits for them, and re-layouts  6.21 us (3%)
    all_to_all x6, starting transfers between devices, copy_for_each(): return lax.all_to_all(copies, axis, split_axis=0, concat_axis=0, tiled=True)  43.5 us
    all_to_all x6, waiting for transfers between devices, copy_for_each(): return lax.all_to_all(copies, axis, split_axis=0, concat_axis=0, tiled=True)  41.9 us
    ppermute x6, starting transfers between devices, shifted(): lax.ppermute(value, axis, [(source, source + steps) for source in range(i...  30.4 us
    dot_general x6, matrix products, shards(): jnp.dot(block[1], rotate(fields[which]), preferred_element_type=jnp.float32)  18.4 us
    dot_general x6, matrix products, shards(): jnp.dot(block[0], fields[which], preferred_element_type=jnp.float32)  16.8 us
    dot_general x6, matrix products, shards(): lax.dot_general(expansion[0, which], coupled[which], (((0,), (0,)), ((),...  11.2 us
    ppermute x6, waiting for transfers between devices, shifted(): lax.ppermute(value, axis, [(source, source + steps) for source in range(i...  10.9 us
    neg x12, other arithmetic, rotate(): return jnp.concatenate([-field[..., half:], field[..., :half]], axis=-1)  6.01 us
  transfers between devices with their start and end apart: 12, of which 10 were waited for; matrix products, arithmetic and copies ran while one was open for 25% of the time, Pallas kernels for 0%

commit v1 on v0

v1 whole, which is shorter than its diff:
```python
import jax
import jax.numpy as jnp
from jax import lax
from jax.experimental import pallas as pl
from jax.experimental.pallas import tpu as pltpu
from jax.sharding import PartitionSpec as P

ITERS = 3
NX, NZ = 4, 8
CHUNKS = 4
MESH = pl.DeviceIdType.MESH


def combine(stacked):
    rows, half = stacked.shape[0] // 2, stacked.shape[1] // 2
    top, low = stacked[:rows], stacked[rows:]
    return jnp.concatenate([top[:, :half] - low[:, half:], top[:, half:] + low[:, :half]], axis=1)


def kernel(
    src_up, src_dn, dg_up, dg_dn, proj, expn, coup, out_up, out_dn,
    s_v, diag_v, proj_v, exp_v, etr, cblk, ag, bv, arr, psend, prec, v_v,
    ld, dld, c_s, c_r, e_s, e_r, ag_s, ag_r, bv_s, bv_r, p_s, p_r,
):
    g = lax.axis_index("layer")
    t = lax.axis_index("trace")
    layers = lax.axis_size("layer")
    x, z = lax.div(t, NZ), lax.rem(t, NZ)
    points, cols = s_v.shape[1:]
    k_own = proj_v.shape[1]
    kc = NZ * k_own
    rows = points // CHUNKS
    sends = (g < layers - 1, g > 0)
    takes = (g > 0, g < layers - 1)
    step = (1, -1)
    outs = (out_up, out_dn)

    def at(gg, xx, zz):
        return (gg, xx * NZ + zz)

    loads = [
        pltpu.make_async_copy(src_up.at[0], s_v.at[0], ld.at[0]),
        pltpu.make_async_copy(src_dn.at[0], s_v.at[1], ld.at[1]),
        pltpu.make_async_copy(proj.at[0], proj_v, ld.at[2]),
        pltpu.make_async_copy(
            coup.at[0, :, :, :, pl.ds(pl.multiple_of(x * kc, kc), kc)], cblk.at[:, x], ld.at[3]
        ),
    ]
    for copy in loads:
        copy.start()

    def diag_load(d, c):
        src = (dg_up, dg_dn)[d]
        return pltpu.make_async_copy(
            src.at[0, :, pl.ds(c * rows, rows), :], diag_v.at[d, c], dld.at[d, c]
        )

    for c in range(CHUNKS):
        for d in range(2):
            diag_load(d, c).start()

    barrier = pltpu.get_barrier_semaphore()
    for dz in range(1, NZ):
        pl.semaphore_signal(barrier, inc=1, device_id=at(g, x, lax.rem(z + dz, NZ)), device_id_type=MESH)
    for dx in range(1, NX):
        pl.semaphore_signal(barrier, inc=1, device_id=at(g, lax.rem(x + dx, NX), z), device_id_type=MESH)
    for d in range(2):
        @pl.when(sends[d])
        def _():
            for dx in range(NX):
                pl.semaphore_signal(
                    barrier, inc=1, device_id=at(g + step[d], lax.rem(x + dx, NX), z), device_id_type=MESH
                )

    loads[0].wait()
    loads[1].wait()
    loads[2].wait()
    zrow = pl.ds(pl.multiple_of(z * k_own, k_own), k_own)

    def coeffs(k, d, field):
        c = jnp.dot(proj_v[d], field[...], preferred_element_type=jnp.float32)
        ag[k, d, zrow, :] = c.astype(jnp.bfloat16)

    def gather_copy(k, d, dz):
        return pltpu.make_async_remote_copy(
            src_ref=ag.at[k, d, zrow, :],
            dst_ref=ag.at[k, d, zrow, :],
            send_sem=ag_s.at[k, d, dz - 1],
            recv_sem=ag_r.at[k, d, dz - 1],
            device_id=at(g, x, lax.rem(z + dz, NZ)),
            device_id_type=MESH,
        )

    far_first = sorted(range(1, NZ), key=lambda dz: -min(dz, NZ - dz))

    def gather_start(k, d):
        for dz in far_first:
            gather_copy(k, d, dz).start()

    for d in range(2):
        @pl.when(sends[d])
        def _():
            coeffs(0, d, s_v.at[d])

    ends = (g > 0).astype(jnp.int32) + (g < layers - 1).astype(jnp.int32)
    pl.semaphore_wait(barrier, NZ - 1 + NX - 1 + NX * ends)

    for d in range(2):
        @pl.when(sends[d])
        def _():
            gather_start(0, d)

    def coupling_copy(dx):
        to = lax.rem(x + dx, NX)
        return pltpu.make_async_remote_copy(
            src_ref=coup.at[0, :, :, :, pl.ds(pl.multiple_of(to * kc, kc), kc)],
            dst_ref=cblk.at[:, x],
            send_sem=c_s.at[dx - 1],
            recv_sem=c_r.at[dx - 1],
            device_id=at(g, to, z),
            device_id_type=MESH,
        )

    for dx in range(1, NX):
        coupling_copy(dx).start()

    def expansion_copy(d):
        return pltpu.make_async_remote_copy(
            src_ref=expn.at[0, d],
            dst_ref=exp_v.at[d],
            send_sem=e_s.at[d],
            recv_sem=e_r.at[d],
            device_id=at(g + step[d], x, z),
            device_id_type=MESH,
        )

    for d in range(2):
        @pl.when(sends[d])
        def _():
            expansion_copy(d).start()

    def dense_copy(k, d, c):
        part = pl.ds(pl.multiple_of(c * rows, rows), rows)
        return pltpu.make_async_remote_copy(
            src_ref=bv.at[k, d, part, :],
            dst_ref=arr.at[k, d, part, :],
            send_sem=bv_s.at[k, d, c],
            recv_sem=bv_r.at[k, d, c],
            device_id=at(g + step[d], x, z),
            device_id_type=MESH,
        )

    def partial_copy(k, d, dx):
        to = lax.rem(x + dx, NX)
        return pltpu.make_async_remote_copy(
            src_ref=psend.at[k, d, to],
            dst_ref=prec.at[k, d, x],
            send_sem=p_s.at[k, d, dx],
            recv_sem=p_r.at[k, d, dx],
            device_id=at(g + step[d], to, z),
            device_id_type=MESH,
        )

    def dense(k, d, c, field):
        part = pl.ds(pl.multiple_of(c * rows, rows), rows)
        both = diag_v[d, c].reshape(2 * rows, points)
        y = jnp.dot(both, field[...], preferred_element_type=jnp.float32)
        bv[k, d, part, :] = combine(y).astype(jnp.bfloat16)
        dense_copy(k, d, c).start()

    def couple(k, d):
        for dz in range(1, NZ):
            gather_copy(k, d, dz).wait_recv()
        gathered = ag[k, d]
        for to in range(NX):
            block = cblk[d, to].reshape(2 * k_own, kc)
            y = jnp.dot(block, gathered, preferred_element_type=jnp.float32)
            psend[k, d, to] = combine(y).astype(jnp.bfloat16)
        for dx in sorted(range(NX), key=lambda dx: -min(dx, NX - dx)):
            partial_copy(k, d, dx).start()

    def assemble(k, d, into):
        for dx in range(NX):
            partial_copy(k, d, dx).wait_recv()
        total = prec[k, d, 0].astype(jnp.float32)
        for xx in range(1, NX):
            total = total + prec[k, d, xx].astype(jnp.float32)
        coupled = total.astype(jnp.bfloat16)

        def one(c, carry):
            part = pl.ds(pl.multiple_of(c * rows, rows), rows)
            dense_copy(k, d, c).wait_recv()
            y = jnp.dot(etr[d, part, :], coupled, preferred_element_type=jnp.float32)
            y = y + arr[k, d, part, :].astype(jnp.float32) + s_v[d, part, :].astype(jnp.float32)
            into[part, :] = y.astype(jnp.bfloat16)
            return carry

        lax.fori_loop(0, CHUNKS, one, 0)

    for k in range(ITERS):
        fields = (s_v.at[0], s_v.at[1]) if k == 0 else (v_v.at[0], v_v.at[1])

        def chunk(c, carry):
            for d in range(2):
                if k == 0:
                    diag_load(d, c).wait()

                @pl.when(sends[d])
                def _():
                    dense(k, d, c, fields[d])

            return carry

        lax.fori_loop(0, CHUNKS, chunk, 0)
        if k == 0:
            loads[3].wait()
            for dx in range(1, NX):
                coupling_copy(dx).wait_recv()
            for d in range(2):
                @pl.when(takes[d])
                def _():
                    expansion_copy(d).wait_recv()
                    etr[d] = exp_v[d].astype(jnp.float32).T.astype(jnp.bfloat16)

        for d in range(2):
            @pl.when(sends[d])
            def _():
                couple(k, d)

        for d in range(2):
            into = outs[d].at[0] if k == ITERS - 1 else v_v.at[d]

            @pl.when(takes[d])
            def _():
                assemble(k, d, into)

            if k == ITERS - 1 or k == 0:
                @pl.when(jnp.logical_not(takes[d]))
                def _():
                    into[...] = s_v[d]

            if k < ITERS - 1:
                @pl.when(sends[d])
                def _():
                    coeffs(k + 1, d, v_v.at[d])
                    gather_start(k + 1, d)

    for dx in range(1, NX):
        coupling_copy(dx).wait_send()
    for d in range(2):
        @pl.when(sends[d])
        def _():
            expansion_copy(d).wait_send()
            for k in range(ITERS):
                for dz in range(1, NZ):
                    gather_copy(k, d, dz).wait_send()
                for c in range(CHUNKS):
                    dense_copy(k, d, c).wait_send()
                for dx in range(NX):
                    partial_copy(k, d, dx).wait_send()


def shards(source_up, source_down, diag_up, diag_down, projection, expansion, coupling):
    points, cols = source_up.shape[1:]
    k_own = projection.shape[2]
    kc = NZ * k_own
    rows = points // CHUNKS
    bf = jnp.bfloat16
    sem = pltpu.SemaphoreType.DMA
    hbm = pl.BlockSpec(memory_space=pl.ANY)
    vmem = pl.BlockSpec(memory_space=pltpu.VMEM)
    return pl.pallas_call(
        kernel,
        out_shape=(
            jax.ShapeDtypeStruct(source_up.shape, bf),
            jax.ShapeDtypeStruct(source_down.shape, bf),
        ),
        in_specs=[hbm] * 7,
        out_specs=(vmem, vmem),
        scratch_shapes=[
            pltpu.VMEM((2, points, cols), bf),
            pltpu.VMEM((2, CHUNKS, 2, rows, points), bf),
            pltpu.VMEM((2, k_own, points), bf),
            pltpu.VMEM((2, k_own, points), bf),
            pltpu.VMEM((2, points, k_own), bf),
            pltpu.VMEM((2, NX, 2, k_own, kc), bf),
            pltpu.VMEM((ITERS, 2, kc, cols), bf),
            pltpu.VMEM((ITERS, 2, points, cols), bf),
            pltpu.VMEM((ITERS, 2, points, cols), bf),
            pltpu.VMEM((ITERS, 2, NX, k_own, cols), bf),
            pltpu.VMEM((ITERS, 2, NX, k_own, cols), bf),
            pltpu.VMEM((2, points, cols), bf),
            sem((4,)),
            sem((2, CHUNKS)),
            sem((NX - 1,)),
            sem((NX - 1,)),
            sem((2,)),
            sem((2,)),
            sem((ITERS, 2, NZ - 1)),
            sem((ITERS, 2, NZ - 1)),
            sem((ITERS, 2, CHUNKS)),
            sem((ITERS, 2, CHUNKS)),
            sem((ITERS, 2, NX)),
            sem((ITERS, 2, NX)),
        ],
        compiler_params=pltpu.CompilerParams(
            collective_id=0, has_side_effects=True, vmem_limit_bytes=60 * 1024 * 1024
        ),
        name="traces",
    )(source_up, source_down, diag_up, diag_down, projection, expansion, coupling)


def solution(mesh):
    return jax.shard_map(
        shards,
        mesh=mesh,
        in_specs=(
            P("layer", "trace", None),
            P("layer", "trace", None),
            P("layer", None, "trace", None),
            P("layer", None, "trace", None),
            P("layer", None, None, "trace"),
            P("layer", None, None, "trace"),
            P("layer", None, None, "trace", None),
        ),
        out_specs=(P("layer", "trace", None), P("layer", "trace", None)),
        check_vma=False,
    )
```

time: 200 us -> 51.8 us (0.26)
  the two profiles are of different devices: /device:TPU:9 before, /device:TPU:1 now
where the time goes in v1:
time: 51.8 us; the launch traced here: 51.6 us
  Pallas kernels  47.3 us (91%)
  local copies, waits for them, and re-layouts  3.74 us (7%)
  between operations  0.64 us (1%)
    pallas_call x1, Pallas kernels, shards(): pl.pallas_call(kernel, out_shape=(jax.ShapeDtypeStruct(source_up.shape, b...  47.3 us
    unnamed x2, local copies, waits for them, and re-layouts  3.74 us

profile of v1, /device:TPU:1, one launch (start us, length us, event | category | flops | bytes accessed | tf_op | source)
XLA Modules:
  0.0 51.6 jit_solution(10622432488094232391)
XLA Ops:
  0.6 47.3 %traces.1 = (bf16[1,1024,256]{2,1,0:T(8,128)(2,1)}, bf16[1,1024,256]{2,1,0:T(8,128)(2,1)}) custom-call(bf16[1,1024,256]{2,1,0:T(8,128)(2,1)} %src_up.1, bf16[1,1024,256]{2,1,0:T(8,128)(2,1)} %src_dn.1, bf16[1,2,1024,1024]{3,2,1,0:T(8,128)(2,1)} %dg_up.1, bf16[1,2,1024,1024]{3,2,1,0:T(8,128)(2,1)} %dg_dn.1, bf16[1,2,32,1024]{3,2,1,0:T(8,128)(2,1)} %proj.1, ...), custom_call_target="tpu_custom_call" | custom-call | tf_op jit(solution)/shard_map/traces/pallas_call | solution.py:272
  47.9 1.9 %copy.11 = bf16[1,1024,256]{2,1,0:T(8,128)(2,1)} copy(bf16[1,1024,256]{2,1,0:T(8,128)(2,1)} %get-tuple-element.4) | data formatting | bytes 1048576
  49.8 1.9 %copy.12 = bf16[1,1024,256]{2,1,0:T(8,128)(2,1)} copy(bf16[1,1024,256]{2,1,0:T(8,128)(2,1)} %get-tuple-element.5) | data formatting | bytes 1048576

commit v2 on v1

v2 whole, which is shorter than its diff:
```python
import jax
import jax.numpy as jnp
from jax import lax
from jax.experimental import pallas as pl
from jax.experimental.pallas import tpu as pltpu
from jax.sharding import PartitionSpec as P

ITERS = 3
NX, NZ = 4, 8
CHUNKS = 4
MESH = pl.DeviceIdType.MESH


def combine(stacked):
    rows, half = stacked.shape[0] // 2, stacked.shape[1] // 2
    top, low = stacked[:rows], stacked[rows:]
    return jnp.concatenate([top[:, :half] - low[:, half:], top[:, half:] + low[:, :half]], axis=1)


def kernel(
    src_up, src_dn, dg_up, dg_dn, proj, expn, coup, out,
    s_v, diag_v, proj_v, exp_v, etr, small, base, cblk, ag, bv, arr, psend, prec, cpl, v_v,
    ld, dld, c_s, c_r, e_s, e_r, ag_s, ag_r, bv_s, bv_r, p_s, p_r,
):
    g = lax.axis_index("layer")
    t = lax.axis_index("trace")
    layers = lax.axis_size("layer")
    x, z = lax.div(t, NZ), lax.rem(t, NZ)
    points, cols = s_v.shape[1:]
    k_own = proj_v.shape[1]
    kc = NZ * k_own
    rows = points // CHUNKS
    first, second = 0, 1
    order = (first, second)
    f32, bf16 = jnp.float32, jnp.bfloat16

    def at(gg, xx, zz):
        return (gg, xx * NZ + zz)

    def ahead(d):
        return g + 1 - 2 * d

    def sends(d):
        return jnp.logical_and(ahead(d) >= 0, ahead(d) < layers)

    def takes(d):
        behind = g - 1 + 2 * d
        return jnp.logical_and(behind >= 0, behind < layers)

    loads = [
        pltpu.make_async_copy(proj.at[0], proj_v, ld.at[2]),
        pltpu.make_async_copy(src_up.at[0], s_v.at[0], ld.at[0]),
        pltpu.make_async_copy(src_dn.at[0], s_v.at[1], ld.at[1]),
        pltpu.make_async_copy(
            coup.at[0, :, :, :, pl.ds(pl.multiple_of(x * kc, kc), kc)], cblk.at[:, x], ld.at[3]
        ),
    ]
    for copy in loads:
        copy.start()

    barrier = pltpu.get_barrier_semaphore()
    for dz in range(1, NZ):
        pl.semaphore_signal(barrier, inc=1, device_id=at(g, x, lax.rem(z + dz, NZ)), device_id_type=MESH)
    for dx in range(1, NX):
        pl.semaphore_signal(barrier, inc=1, device_id=at(g, lax.rem(x + dx, NX), z), device_id_type=MESH)
    for d in range(2):
        @pl.when(sends(d))
        def _():
            for dx in range(NX):
                pl.semaphore_signal(
                    barrier, inc=1, device_id=at(ahead(d), lax.rem(x + dx, NX), z), device_id_type=MESH
                )

    def diag_load(d, c):
        src = (dg_up, dg_dn)[d]
        return pltpu.make_async_copy(
            src.at[0, :, pl.ds(c * rows, rows), :], diag_v.at[d, c], dld.at[d, c]
        )

    def diag_start(d):
        for c in range(CHUNKS):
            diag_load(d, c).start()

    diag_start(0)
    diag_start(1)

    for copy in loads[:3]:
        copy.wait()
    zrow = pl.ds(pl.multiple_of(z * k_own, k_own), k_own)

    def gather_copy(k, d, dz):
        return pltpu.make_async_remote_copy(
            src_ref=ag.at[k, d, zrow, :],
            dst_ref=ag.at[k, d, zrow, :],
            send_sem=ag_s.at[k, d, dz - 1],
            recv_sem=ag_r.at[k, d, dz - 1],
            device_id=at(g, x, lax.rem(z + dz, NZ)),
            device_id_type=MESH,
        )

    def far_first(count, start):
        return sorted(range(start, count), key=lambda step: -min(step, count - step))

    def gather_start(k, d):
        for dz in far_first(NZ, 1):
            gather_copy(k, d, dz).start()

    for d in range(2):
        @pl.when(sends(d))
        def _():
            c = jnp.dot(proj_v[d], s_v[d], preferred_element_type=f32)
            ag[0, d, zrow, :] = c.astype(bf16)

        @pl.when(jnp.logical_not(takes(d)))
        def _():
            v_v[d] = s_v[d]

    ends = (g > 0).astype(jnp.int32) + (g < layers - 1).astype(jnp.int32)
    pl.semaphore_wait(barrier, NZ - 1 + NX - 1 + NX * ends)

    for d in order:
        @pl.when(sends(d))
        def _():
            gather_start(0, d)

    def coupling_copy(dx):
        to = lax.rem(x + dx, NX)
        return pltpu.make_async_remote_copy(
            src_ref=coup.at[0, :, :, :, pl.ds(pl.multiple_of(to * kc, kc), kc)],
            dst_ref=cblk.at[:, x],
            send_sem=c_s.at[dx - 1],
            recv_sem=c_r.at[dx - 1],
            device_id=at(g, to, z),
            device_id_type=MESH,
        )

    for dx in far_first(NX, 1):
        coupling_copy(dx).start()

    def expansion_copy(d):
        return pltpu.make_async_remote_copy(
            src_ref=expn.at[0, d],
            dst_ref=exp_v.at[d],
            send_sem=e_s.at[d],
            recv_sem=e_r.at[d],
            device_id=at(ahead(d), x, z),
            device_id_type=MESH,
        )

    for d in range(2):
        @pl.when(sends(d))
        def _():
            expansion_copy(d).start()

    def part_of(c):
        return pl.ds(pl.multiple_of(c * rows, rows), rows)

    def dense_copy(k, d, c):
        return pltpu.make_async_remote_copy(
            src_ref=bv.at[k, d, part_of(c), :],
            dst_ref=arr.at[k, d, part_of(c), :],
            send_sem=bv_s.at[k, d, c],
            recv_sem=bv_r.at[k, d, c],
            device_id=at(ahead(d), x, z),
            device_id_type=MESH,
        )

    def partial_copy(k, d, dx):
        to = lax.rem(x + dx, NX)
        return pltpu.make_async_remote_copy(
            src_ref=psend.at[k, d, to],
            dst_ref=prec.at[k, d, x],
            send_sem=p_s.at[k, d, dx],
            recv_sem=p_r.at[k, d, dx],
            device_id=at(ahead(d), to, z),
            device_id_type=MESH,
        )

    def dense(k, d, c0, c1):
        @pl.when(sends(d))
        def _():
            def one(c, carry):
                both = diag_v[d, c].reshape(2 * rows, points)
                field = s_v[d] if k == 0 else v_v[d]
                y = jnp.dot(both, field, preferred_element_type=f32)
                bv[k, d, part_of(c), :] = combine(y).astype(bf16)
                dense_copy(k, d, c).start()
                return carry

            if k == 0:
                for c in range(c0, c1):
                    pltpu.make_async_copy(diag_v.at[d, c], diag_v.at[d, c], dld.at[d, c]).wait()
                    one(c, 0)
            else:
                lax.fori_loop(c0, c1, one, 0)

        if k == 0:
            @pl.when(jnp.logical_not(sends(d)))
            def _():
                for c in range(c0, c1):
                    pltpu.make_async_copy(diag_v.at[d, c], diag_v.at[d, c], dld.at[d, c]).wait()

    def couple(k, d):
        @pl.when(sends(d))
        def _():
            for dz in range(1, NZ):
                gather_copy(k, d, dz).wait_recv()
            y = jnp.dot(cblk[d].reshape(NX * 2 * k_own, kc), ag[k, d], preferred_element_type=f32)
            for to in range(NX):
                psend[k, d, to] = combine(y[to * 2 * k_own : (to + 1) * 2 * k_own]).astype(bf16)
            for dx in far_first(NX, 0):
                partial_copy(k, d, dx).start()

    def arrivals(k, d):
        @pl.when(takes(d))
        def _():
            total = jnp.zeros((k_own, cols), f32)
            for c in range(CHUNKS):
                dense_copy(k, d, c).wait_recv()
                part = pl.ds(c * rows, rows)
                field = s_v[d, part, :].astype(f32) + arr[k, d, part, :].astype(f32)
                total = total + jnp.dot(proj_v[d, :, part], field.astype(bf16), preferred_element_type=f32)
            base[d] = total

    def coupled_sum(k, d):
        for dx in range(NX):
            partial_copy(k, d, dx).wait_recv()
        total = prec[k, d, 0].astype(f32)
        for xx in range(1, NX):
            total = total + prec[k, d, xx].astype(f32)
        coupled = total.astype(bf16)
        cpl[d] = coupled
        return coupled

    def coeffs(k, d):
        @pl.when(takes(d))
        def _():
            coupled = coupled_sum(k - 1, d)
            c = base[d] + jnp.dot(small[d], coupled, preferred_element_type=f32)
            ag[k, d, zrow, :] = c.astype(bf16)

        @pl.when(jnp.logical_not(takes(d)))
        def _():
            ag[k, d, zrow, :] = ag[0, d, zrow, :]

        @pl.when(sends(d))
        def _():
            gather_start(k, d)

    def assemble(k, d, into):
        def one(c, carry):
            part = part_of(c)
            if k == ITERS - 1:
                dense_copy(k, d, c).wait_recv()
            y = jnp.dot(etr[d, part, :], cpl[d], preferred_element_type=f32)
            y = y + arr[k, d, part, :].astype(f32) + s_v[d, part, :].astype(f32)
            into[part, :] = y.astype(bf16)
            return carry

        @pl.when(takes(d))
        def _():
            if k == ITERS - 1:
                coupled_sum(k, d)
            lax.fori_loop(0, CHUNKS, one, 0)

    half = CHUNKS // 2
    dense(0, first, 0, CHUNKS)
    dense(0, second, 0, CHUNKS)
    for d in order:
        @pl.when(takes(d))
        def _():
            expansion_copy(d).wait_recv()
            etr[d] = exp_v[d].astype(f32).T.astype(bf16)
            small[d] = lax.dot_general(
                proj_v[d], exp_v[d], (((1,), (1,)), ((), ())), preferred_element_type=f32
            ).astype(bf16)
    loads[3].wait()
    for dx in range(1, NX):
        coupling_copy(dx).wait_recv()
    couple(0, first)
    couple(0, second)
    for k in range(1, ITERS):
        arrivals(k - 1, first)
        coeffs(k, first)
        assemble(k - 1, first, v_v.at[first])
        dense(k, first, 0, half)
        arrivals(k - 1, second)
        coeffs(k, second)
        dense(k, first, half, CHUNKS)
        assemble(k - 1, second, v_v.at[second])
        dense(k, second, 0, half)
        couple(k, first)
        dense(k, second, half, CHUNKS)
        couple(k, second)
    for d in order:
        assemble(ITERS - 1, d, out.at[d])

        @pl.when(jnp.logical_not(takes(d)))
        def _():
            out[d] = s_v[d]

    for dx in range(1, NX):
        coupling_copy(dx).wait_send()
    for d in range(2):
        @pl.when(sends(d))
        def _():
            expansion_copy(d).wait_send()
            for k in range(ITERS):
                for dz in range(1, NZ):
                    gather_copy(k, d, dz).wait_send()
                for c in range(CHUNKS):
                    dense_copy(k, d, c).wait_send()
                for dx in range(NX):
                    partial_copy(k, d, dx).wait_send()


def write_out(both, out_up, out_dn, sem):
    copies = [
        pltpu.make_async_copy(both.at[d], out.at[0], sem.at[d])
        for d, out in enumerate((out_up, out_dn))
    ]
    for copy in copies:
        copy.start()
    for copy in copies:
        copy.wait()


def shards(source_up, source_down, diag_up, diag_down, projection, expansion, coupling):
    points, cols = source_up.shape[1:]
    k_own = projection.shape[2]
    kc = NZ * k_own
    rows = points // CHUNKS
    bf = jnp.bfloat16
    sem = pltpu.SemaphoreType.DMA
    hbm = pl.BlockSpec(memory_space=pl.ANY)
    vmem = pl.BlockSpec(memory_space=pltpu.VMEM)
    both = pl.pallas_call(
        kernel,
        out_shape=pltpu.VMEM((2, points, cols), bf),
        in_specs=[pl.BlockSpec(memory_space=pltpu.HBM)] * 7,
        out_specs=vmem,
        scratch_shapes=[
            pltpu.VMEM((2, points, cols), bf),
            pltpu.VMEM((2, CHUNKS, 2, rows, points), bf),
            pltpu.VMEM((2, k_own, points), bf),
            pltpu.VMEM((2, k_own, points), bf),
            pltpu.VMEM((2, points, k_own), bf),
            pltpu.VMEM((2, k_own, k_own), bf),
            pltpu.VMEM((2, k_own, cols), jnp.float32),
            pltpu.VMEM((2, NX, 2, k_own, kc), bf),
            pltpu.VMEM((ITERS, 2, kc, cols), bf),
            pltpu.VMEM((ITERS, 2, points, cols), bf),
            pltpu.VMEM((ITERS, 2, points, cols), bf),
            pltpu.VMEM((ITERS, 2, NX, k_own, cols), bf),
            pltpu.VMEM((ITERS, 2, NX, k_own, cols), bf),
            pltpu.VMEM((2, k_own, cols), bf),
            pltpu.VMEM((2, points, cols), bf),
            sem((4,)),
            sem((2, CHUNKS)),
            sem((NX - 1,)),
            sem((NX - 1,)),
            sem((2,)),
            sem((2,)),
            sem((ITERS, 2, NZ - 1)),
            sem((ITERS, 2, NZ - 1)),
            sem((ITERS, 2, CHUNKS)),
            sem((ITERS, 2, CHUNKS)),
            sem((ITERS, 2, NX)),
            sem((ITERS, 2, NX)),
        ],
        compiler_params=pltpu.CompilerParams(
            collective_id=0, has_side_effects=True, vmem_limit_bytes=67043328 - (1 << 20)
        ),
        name="traces",
    )(source_up, source_down, diag_up, diag_down, projection, expansion, coupling)
    return pl.pallas_call(
        write_out,
        out_shape=(
            jax.ShapeDtypeStruct(source_up.shape, bf),
            jax.ShapeDtypeStruct(source_down.shape, bf),
        ),
        in_specs=[vmem],
        out_specs=(hbm, hbm),
        scratch_shapes=[sem((2,))],
        compiler_params=pltpu.CompilerParams(vmem_limit_bytes=4 * 1024 * 1024),
        name="write_out",
    )(both)


def solution(mesh):
    return jax.shard_map(
        shards,
        mesh=mesh,
        in_specs=(
            P("layer", "trace", None),
            P("layer", "trace", None),
            P("layer", None, "trace", None),
            P("layer", None, "trace", None),
            P("layer", None, None, "trace"),
            P("layer", None, None, "trace"),
            P("layer", None, None, "trace", None),
        ),
        out_specs=(P("layer", "trace", None), P("layer", "trace", None)),
        check_vma=False,
    )
```

time: 51.8 us -> 46.3 us (0.89)
  the two profiles are of different devices: /device:TPU:1 before, /device:TPU:9 now
where the time goes in v2:
time: 46.3 us; the launch traced here: 45.4 us
  Pallas kernels  44.8 us (97%)
  between operations  0.64 us (1%)
    pallas_call x1, Pallas kernels, shards(): pl.pallas_call(kernel, out_shape=pltpu.VMEM((2, points, cols), bf), in_sp...  43.8 us
    pallas_call x1, Pallas kernels, shards(): pl.pallas_call(write_out, out_shape=(jax.ShapeDtypeStruct(source_up.shape...  0.99 us

profile of v2, /device:TPU:9, one launch (start us, length us, event | category | flops | bytes accessed | tf_op | source)
XLA Modules:
  0.0 45.4 jit_solution(13889958933131829189)
XLA Ops:
  0.6 43.8 %traces.1.both = bf16[2,1024,256]{2,1,0:T(8,128)(2,1)S(1)} custom-call(bf16[1,1024,256]{2,1,0:T(8,128)(2,1)} %src_up.1, bf16[1,1024,256]{2,1,0:T(8,128)(2,1)} %src_dn.1, bf16[1,2,1024,1024]{3,2,1,0:T(8,128)(2,1)} %dg_up.1, bf16[1,2,1024,1024]{3,2,1,0:T(8,128)(2,1)} %dg_dn.1, bf16[1,2,32,1024]{3,2,1,0:T(8,128)(2,1)} %proj.1, bf16[1,2,32,1024]{3,2,1,0:T(8,128)(2,1)} %expn.1, ...), custom_call_target="tpu_custom_call" | custom-call | tf_op jit(solution)/shard_map/traces/pallas_call | solution.py:337
  44.4 1.0 %write_out.1 = (bf16[1,1024,256]{2,1,0:T(8,128)(2,1)}, bf16[1,1024,256]{2,1,0:T(8,128)(2,1)}) custom-call(bf16[2,1024,256]{2,1,0:T(8,128)(2,1)S(1)} %traces.1.both), custom_call_target="tpu_custom_call" | custom-call | tf_op jit(solution)/shard_map/write_out/pallas_call | solution.py:376

commit v3 on v2

--- a/solution.py
+++ b/solution.py
@@ -7,6 +7,7 @@
 
 ITERS = 3
 NX, NZ = 4, 8
+PIECES = 4
 CHUNKS = 4
 MESH = pl.DeviceIdType.MESH
 
@@ -19,7 +20,7 @@
 
 def kernel(
     src_up, src_dn, dg_up, dg_dn, proj, expn, coup, out,
-    s_v, diag_v, proj_v, exp_v, etr, small, base, cblk, ag, bv, arr, psend, prec, cpl, v_v,
+    s_v, diag_v, proj_v, exp_v, etr, small, base, cblk, ag, bv, arr, psend, prec, v_v,
     ld, dld, c_s, c_r, e_s, e_r, ag_s, ag_r, bv_s, bv_r, p_s, p_r,
 ):
     g = lax.axis_index("layer")
@@ -30,8 +31,12 @@
     k_own = proj_v.shape[1]
     kc = NZ * k_own
     rows = points // CHUNKS
-    first, second = 0, 1
-    order = (first, second)
+
+    def order_at(k):
+        second = lax.rem(g + k, 2)
+        return 1 - second, second
+
+    first, second = order = order_at(0)
     f32, bf16 = jnp.float32, jnp.bfloat16
 
     def at(gg, xx, zz):
@@ -81,11 +86,18 @@
         for c in range(CHUNKS):
             diag_load(d, c).start()
 
-    diag_start(0)
-    diag_start(1)
-
     for copy in loads[:3]:
         copy.wait()
+    @pl.when(first == 0)
+    def _():
+        diag_start(0)
+        diag_start(1)
+
+    @pl.when(first == 1)
+    def _():
+        diag_start(1)
+        diag_start(0)
+
     zrow = pl.ds(pl.multiple_of(z * k_own, k_own), k_own)
 
     def gather_copy(k, d, dz):
@@ -105,15 +117,15 @@
         for dz in far_first(NZ, 1):
             gather_copy(k, d, dz).start()
 
-    for d in range(2):
-        @pl.when(sends(d))
-        def _():
-            c = jnp.dot(proj_v[d], s_v[d], preferred_element_type=f32)
-            ag[0, d, zrow, :] = c.astype(bf16)
-
-        @pl.when(jnp.logical_not(takes(d)))
-        def _():
-            v_v[d] = s_v[d]
+    def start(d, carry):
+        c = jnp.dot(proj_v[d], s_v[d], preferred_element_type=f32)
+        ag[0, d, zrow, :] = c.astype(bf16)
+        return carry
+
+    lax.fori_loop(0, 2, start, 0)
+    field_copies = [pltpu.make_async_copy(s_v.at[d], v_v.at[d], ld.at[4 + d]) for d in range(2)]
+    for copy in field_copies:
+        copy.start()
 
     ends = (g > 0).astype(jnp.int32) + (g < layers - 1).astype(jnp.int32)
     pl.semaphore_wait(barrier, NZ - 1 + NX - 1 + NX * ends)
@@ -177,28 +189,21 @@
         )
 
     def dense(k, d, c0, c1):
-        @pl.when(sends(d))
-        def _():
-            def one(c, carry):
+        def one(c, carry):
+            @pl.when(k == 0)
+            def _():
+                pltpu.make_async_copy(diag_v.at[d, c], diag_v.at[d, c], dld.at[d, c]).wait()
+
+            @pl.when(sends(d))
+            def _():
                 both = diag_v[d, c].reshape(2 * rows, points)
-                field = s_v[d] if k == 0 else v_v[d]
-                y = jnp.dot(both, field, preferred_element_type=f32)
+                y = jnp.dot(both, v_v[d], preferred_element_type=f32)
                 bv[k, d, part_of(c), :] = combine(y).astype(bf16)
                 dense_copy(k, d, c).start()
-                return carry
-
-            if k == 0:
-                for c in range(c0, c1):
-                    pltpu.make_async_copy(diag_v.at[d, c], diag_v.at[d, c], dld.at[d, c]).wait()
-                    one(c, 0)
-            else:
-                lax.fori_loop(c0, c1, one, 0)
-
-        if k == 0:
-            @pl.when(jnp.logical_not(sends(d)))
-            def _():
-                for c in range(c0, c1):
-                    pltpu.make_async_copy(diag_v.at[d, c], diag_v.at[d, c], dld.at[d, c]).wait()
+
+            return carry
+
+        lax.fori_loop(c0, c1, one, 0)
 
     def couple(k, d):
         @pl.when(sends(d))
@@ -222,21 +227,22 @@
                 total = total + jnp.dot(proj_v[d, :, part], field.astype(bf16), preferred_element_type=f32)
             base[d] = total
 
-    def coupled_sum(k, d):
+    def partials_wait(k, d):
         for dx in range(NX):
             partial_copy(k, d, dx).wait_recv()
+
+    def coupled_sum(k, d):
         total = prec[k, d, 0].astype(f32)
         for xx in range(1, NX):
             total = total + prec[k, d, xx].astype(f32)
-        coupled = total.astype(bf16)
-        cpl[d] = coupled
-        return coupled
+        return total.astype(bf16)
 
     def coeffs(k, d):
         @pl.when(takes(d))
         def _():
-            coupled = coupled_sum(k - 1, d)
-            c = base[d] + jnp.dot(small[d], coupled, preferred_element_type=f32)
+            partials_wait(k - 1, d)
+            stacked = prec[k - 1, d].reshape(NX * k_own, cols)
+            c = base[d] + jnp.dot(small[d], stacked, preferred_element_type=f32)
             ag[k, d, zrow, :] = c.astype(bf16)
 
         @pl.when(jnp.logical_not(takes(d)))
@@ -248,76 +254,111 @@
             gather_start(k, d)
 
     def assemble(k, d, into):
-        def one(c, carry):
+        def one(c, coupled):
             part = part_of(c)
-            if k == ITERS - 1:
-                dense_copy(k, d, c).wait_recv()
-            y = jnp.dot(etr[d, part, :], cpl[d], preferred_element_type=f32)
+            y = jnp.dot(etr[d, part, :], coupled, preferred_element_type=f32)
             y = y + arr[k, d, part, :].astype(f32) + s_v[d, part, :].astype(f32)
             into[part, :] = y.astype(bf16)
-            return carry
-
-        @pl.when(takes(d))
-        def _():
-            if k == ITERS - 1:
-                coupled_sum(k, d)
-            lax.fori_loop(0, CHUNKS, one, 0)
-
-    half = CHUNKS // 2
-    dense(0, first, 0, CHUNKS)
-    dense(0, second, 0, CHUNKS)
-    for d in order:
-        @pl.when(takes(d))
-        def _():
-            expansion_copy(d).wait_recv()
-            etr[d] = exp_v[d].astype(f32).T.astype(bf16)
-            small[d] = lax.dot_general(
-                proj_v[d], exp_v[d], (((1,), (1,)), ((), ())), preferred_element_type=f32
-            ).astype(bf16)
-    loads[3].wait()
-    for dx in range(1, NX):
-        coupling_copy(dx).wait_recv()
-    couple(0, first)
-    couple(0, second)
-    for k in range(1, ITERS):
-        arrivals(k - 1, first)
-        coeffs(k, first)
-        assemble(k - 1, first, v_v.at[first])
-        dense(k, first, 0, half)
-        arrivals(k - 1, second)
-        coeffs(k, second)
-        dense(k, first, half, CHUNKS)
-        assemble(k - 1, second, v_v.at[second])
+            return coupled
+
+        lax.fori_loop(0, CHUNKS, one, coupled_sum(k, d))
+
+    def advance(k, d):
+        @pl.when(k > 0)
+        def _():
+            arrivals(k - 1, d)
+            coeffs(k, d)
+
+            @pl.when(takes(d))
+            def _():
+                assemble(k - 1, d, v_v.at[d])
+
+    def iteration(k, carry):
+        first, second = order_at(k)
+        advance(k, first)
+        dense(k, first, 0, CHUNKS)
+        advance(k, second)
         dense(k, second, 0, half)
+
+        @pl.when(k == 0)
+        def _():
+            def expansions(d, carry):
+                @pl.when(takes(d))
+                def _():
+                    expansion_copy(d).wait_recv()
+                    etr[d] = exp_v[d].astype(f32).T.astype(bf16)
+                    one = lax.dot_general(
+                        proj_v[d], exp_v[d], (((1,), (1,)), ((), ())), preferred_element_type=f32
+                    )
+                    small[d] = jnp.concatenate([one] * NX, axis=1).astype(bf16)
+
+                return carry
+
+            lax.fori_loop(0, 2, expansions, 0)
+            loads[3].wait()
+            for dx in range(1, NX):
+                coupling_copy(dx).wait_recv()
+
         couple(k, first)
         dense(k, second, half, CHUNKS)
         couple(k, second)
-    for d in order:
-        assemble(ITERS - 1, d, out.at[d])
+        return carry
+
+    half = CHUNKS // 2
+    for copy in field_copies:
+        copy.wait()
+    lax.fori_loop(0, ITERS, iteration, 0)
+
+    def last(turn, carry):
+        d = lax.rem(order_at(ITERS)[0] + turn, 2)
+
+        @pl.when(takes(d))
+        def _():
+            for c in range(CHUNKS):
+                dense_copy(ITERS - 1, d, c).wait_recv()
+            partials_wait(ITERS - 1, d)
+            assemble(ITERS - 1, d, out.at[d])
 
         @pl.when(jnp.logical_not(takes(d)))
         def _():
             out[d] = s_v[d]
+
+        return carry
+
+    lax.fori_loop(0, 2, last, 0)
 
     for dx in range(1, NX):
         coupling_copy(dx).wait_send()
-    for d in range(2):
+
+    def sent(d, carry):
         @pl.when(sends(d))
         def _():
             expansion_copy(d).wait_send()
-            for k in range(ITERS):
+
+            def sent_in(k, carry):
                 for dz in range(1, NZ):
                     gather_copy(k, d, dz).wait_send()
                 for c in range(CHUNKS):
                     dense_copy(k, d, c).wait_send()
                 for dx in range(NX):
                     partial_copy(k, d, dx).wait_send()
+                return carry
+
+            lax.fori_loop(0, ITERS, sent_in, 0)
+
+        return carry
+
+    lax.fori_loop(0, 2, sent, 0)
 
 
 def write_out(both, out_up, out_dn, sem):
+    rows = both.shape[1] // PIECES
     copies = [
-        pltpu.make_async_copy(both.at[d], out.at[0], sem.at[d])
+        pltpu.make_async_copy(
+            both.at[d, pl.ds(i * rows, rows)], out.at[0, pl.ds(i * rows, rows)], sem.at[d, i]
+        )
         for d, out in enumerate((out_up, out_dn))
+        for i in range(PIECES)
     ]
     for copy in copies:
         copy.start()
@@ -345,7 +386,7 @@
             pltpu.VMEM((2, k_own, points), bf),
             pltpu.VMEM((2, k_own, points), bf),
             pltpu.VMEM((2, points, k_own), bf),
-            pltpu.VMEM((2, k_own, k_own), bf),
+            pltpu.VMEM((2, k_own, NX * k_own), bf),
             pltpu.VMEM((2, k_own, cols), jnp.float32),
             pltpu.VMEM((2, NX, 2, k_own, kc), bf),
             pltpu.VMEM((ITERS, 2, kc, cols), bf),
@@ -353,9 +394,8 @@
             pltpu.VMEM((ITERS, 2, points, cols), bf),
             pltpu.VMEM((ITERS, 2, NX, k_own, cols), bf),
             pltpu.VMEM((ITERS, 2, NX, k_own, cols), bf),
-            pltpu.VMEM((2, k_own, cols), bf),
             pltpu.VMEM((2, points, cols), bf),
-            sem((4,)),
+            sem((6,)),
             sem((2, CHUNKS)),
             sem((NX - 1,)),
             sem((NX - 1,)),
@@ -381,7 +421,7 @@
         ),
         in_specs=[vmem],
         out_specs=(hbm, hbm),
-        scratch_shapes=[sem((2,))],
+        scratch_shapes=[sem((2, PIECES))],
         compiler_params=pltpu.CompilerParams(vmem_limit_bytes=4 * 1024 * 1024),
         name="write_out",
     )(both)

time: 46.3 us -> 44.8 us (0.968); the launches traced: 45.4 us -> 44.7 us
  Pallas kernels: 44.8 us -> 44.1 us
    pallas_call x1, Pallas kernels: 43.8 us -> 43 us  [shards(): pl.pallas_call(kernel, out_shape=pltpu.VMEM((2, points, cols), bf), in_sp...]
where the time goes in v3:
time: 44.8 us; the launch traced here: 44.7 us
  Pallas kernels  44.1 us (98%)
  between operations  0.64 us (1%)
    pallas_call x1, Pallas kernels, shards(): pl.pallas_call(kernel, out_shape=pltpu.VMEM((2, points, cols), bf), in_sp...  43 us
    pallas_call x1, Pallas kernels, shards(): pl.pallas_call(write_out, out_shape=(jax.ShapeDtypeStruct(source_up.shape...  1.03 us

profile of v3, /device:TPU:9, one launch (start us, length us, event | category | flops | bytes accessed | tf_op | source)
XLA Modules:
  0.0 44.7 jit_solution(7395086013599049945)
XLA Ops:
  0.6 43.0 %traces.1.both = bf16[2,1024,256]{2,1,0:T(8,128)(2,1)S(1)} custom-call(bf16[1,1024,256]{2,1,0:T(8,128)(2,1)} %src_up.1, bf16[1,1024,256]{2,1,0:T(8,128)(2,1)} %src_dn.1, bf16[1,2,1024,1024]{3,2,1,0:T(8,128)(2,1)} %dg_up.1, bf16[1,2,1024,1024]{3,2,1,0:T(8,128)(2,1)} %dg_dn.1, bf16[1,2,32,1024]{3,2,1,0:T(8,128)(2,1)} %proj.1, bf16[1,2,32,1024]{3,2,1,0:T(8,128)(2,1)} %expn.1, ...), custom_call_target="tpu_custom_call" | custom-call | tf_op jit(solution)/shard_map/traces/pallas_call | solution.py:378
  43.7 1.0 %write_out.1 = (bf16[1,1024,256]{2,1,0:T(8,128)(2,1)}, bf16[1,1024,256]{2,1,0:T(8,128)(2,1)}) custom-call(bf16[2,1024,256]{2,1,0:T(8,128)(2,1)S(1)} %traces.1.both), custom_call_target="tpu_custom_call" | custom-call | tf_op jit(solution)/shard_map/write_out/pallas_call | solution.py:416

commit v4 on v3

--- a/solution.py
+++ b/solution.py
@@ -219,13 +219,10 @@
     def arrivals(k, d):
         @pl.when(takes(d))
         def _():
-            total = jnp.zeros((k_own, cols), f32)
             for c in range(CHUNKS):
                 dense_copy(k, d, c).wait_recv()
-                part = pl.ds(c * rows, rows)
-                field = s_v[d, part, :].astype(f32) + arr[k, d, part, :].astype(f32)
-                total = total + jnp.dot(proj_v[d, :, part], field.astype(bf16), preferred_element_type=f32)
-            base[d] = total
+            field = s_v[d].astype(f32) + arr[k, d].astype(f32)
+            base[d] = jnp.dot(proj_v[d], field.astype(bf16), preferred_element_type=f32)
 
     def partials_wait(k, d):
         for dx in range(NX):
@@ -254,31 +251,33 @@
             gather_start(k, d)
 
     def assemble(k, d, into):
-        def one(c, coupled):
-            part = part_of(c)
+        coupled = coupled_sum(k, d)
+        for c in range(1):
+            part = pl.ds(c * points // 1, points // 1)
             y = jnp.dot(etr[d, part, :], coupled, preferred_element_type=f32)
             y = y + arr[k, d, part, :].astype(f32) + s_v[d, part, :].astype(f32)
             into[part, :] = y.astype(bf16)
-            return coupled
-
-        lax.fori_loop(0, CHUNKS, one, coupled_sum(k, d))
-
-    def advance(k, d):
+
+    def renew(k, d):
         @pl.when(k > 0)
         def _():
             arrivals(k - 1, d)
             coeffs(k, d)
 
-            @pl.when(takes(d))
-            def _():
-                assemble(k - 1, d, v_v.at[d])
+    def advance(k, d):
+        @pl.when(jnp.logical_and(k > 0, takes(d)))
+        def _():
+            assemble(k - 1, d, v_v.at[d])
 
     def iteration(k, carry):
         first, second = order_at(k)
+        renew(k, first)
         advance(k, first)
-        dense(k, first, 0, CHUNKS)
+        dense(k, first, 0, half)
+        renew(k, second)
+        dense(k, first, half, CHUNKS)
         advance(k, second)
-        dense(k, second, 0, half)
+        dense(k, second, 0, CHUNKS)
 
         @pl.when(k == 0)
         def _():
@@ -300,7 +299,6 @@
                 coupling_copy(dx).wait_recv()
 
         couple(k, first)
-        dense(k, second, half, CHUNKS)
         couple(k, second)
         return carry
 

time: 44.8 us -> 43.5 us (0.971)
  Pallas kernels: 44.1 us -> 42.8 us
    pallas_call x1, Pallas kernels: 43 us -> 41.7 us  [shards(): pl.pallas_call(kernel, out_shape=pltpu.VMEM((2, points, cols), bf), in_sp...]
where the time goes in v4:
time: 43.5 us; the launch traced here: 43.4 us
  Pallas kernels  42.8 us (98%)
  between operations  0.64 us (1%)
    pallas_call x1, Pallas kernels, shards(): pl.pallas_call(kernel, out_shape=pltpu.VMEM((2, points, cols), bf), in_sp...  41.7 us
    pallas_call x1, Pallas kernels, shards(): pl.pallas_call(write_out, out_shape=(jax.ShapeDtypeStruct(source_up.shape...  1.03 us

profile of v4, /device:TPU:9, one launch (start us, length us, event | category | flops | bytes accessed | tf_op | source)
XLA Modules:
  0.0 43.4 jit_solution(14227359612604854200)
XLA Ops:
  0.6 41.7 %traces.1.both = bf16[2,1024,256]{2,1,0:T(8,128)(2,1)S(1)} custom-call(bf16[1,1024,256]{2,1,0:T(8,128)(2,1)} %src_up.1, bf16[1,1024,256]{2,1,0:T(8,128)(2,1)} %src_dn.1, bf16[1,2,1024,1024]{3,2,1,0:T(8,128)(2,1)} %dg_up.1, bf16[1,2,1024,1024]{3,2,1,0:T(8,128)(2,1)} %dg_dn.1, bf16[1,2,32,1024]{3,2,1,0:T(8,128)(2,1)} %proj.1, bf16[1,2,32,1024]{3,2,1,0:T(8,128)(2,1)} %expn.1, ...), custom_call_target="tpu_custom_call" | custom-call | tf_op jit(solution)/shard_map/traces/pallas_call | solution.py:376
  42.4 1.0 %write_out.1 = (bf16[1,1024,256]{2,1,0:T(8,128)(2,1)}, bf16[1,1024,256]{2,1,0:T(8,128)(2,1)}) custom-call(bf16[2,1024,256]{2,1,0:T(8,128)(2,1)S(1)} %traces.1.both), custom_call_target="tpu_custom_call" | custom-call | tf_op jit(solution)/shard_map/write_out/pallas_call | solution.py:414

commit v5 on v4

--- a/solution.py
+++ b/solution.py
@@ -8,7 +8,7 @@
 ITERS = 3
 NX, NZ = 4, 8
 PIECES = 4
-CHUNKS = 4
+CHUNKS = 2
 MESH = pl.DeviceIdType.MESH
 
 
@@ -20,7 +20,7 @@
 
 def kernel(
     src_up, src_dn, dg_up, dg_dn, proj, expn, coup, out,
-    s_v, diag_v, proj_v, exp_v, etr, small, base, cblk, ag, bv, arr, psend, prec, v_v,
+    s_v, diag_v, proj_v, exp_v, etr, small, base, cblk, ag, bv, arr, psend, prec, v_v, fixed,
     ld, dld, c_s, c_r, e_s, e_r, ag_s, ag_r, bv_s, bv_r, p_s, p_r,
 ):
     g = lax.axis_index("layer")
@@ -222,6 +222,7 @@
             for c in range(CHUNKS):
                 dense_copy(k, d, c).wait_recv()
             field = s_v[d].astype(f32) + arr[k, d].astype(f32)
+            fixed[d] = field
             base[d] = jnp.dot(proj_v[d], field.astype(bf16), preferred_element_type=f32)
 
     def partials_wait(k, d):
@@ -255,8 +256,7 @@
         for c in range(1):
             part = pl.ds(c * points // 1, points // 1)
             y = jnp.dot(etr[d, part, :], coupled, preferred_element_type=f32)
-            y = y + arr[k, d, part, :].astype(f32) + s_v[d, part, :].astype(f32)
-            into[part, :] = y.astype(bf16)
+            into[part, :] = (y + fixed[d, part, :]).astype(bf16)
 
     def renew(k, d):
         @pl.when(k > 0)
@@ -307,24 +307,6 @@
         copy.wait()
     lax.fori_loop(0, ITERS, iteration, 0)
 
-    def last(turn, carry):
-        d = lax.rem(order_at(ITERS)[0] + turn, 2)
-
-        @pl.when(takes(d))
-        def _():
-            for c in range(CHUNKS):
-                dense_copy(ITERS - 1, d, c).wait_recv()
-            partials_wait(ITERS - 1, d)
-            assemble(ITERS - 1, d, out.at[d])
-
-        @pl.when(jnp.logical_not(takes(d)))
-        def _():
-            out[d] = s_v[d]
-
-        return carry
-
-    lax.fori_loop(0, 2, last, 0)
-
     for dx in range(1, NX):
         coupling_copy(dx).wait_send()
 
@@ -347,6 +329,25 @@
         return carry
 
     lax.fori_loop(0, 2, sent, 0)
+
+    def last(turn, carry):
+        d = lax.rem(order_at(ITERS)[0] + turn, 2)
+
+        @pl.when(takes(d))
+        def _():
+            for c in range(CHUNKS):
+                dense_copy(ITERS - 1, d, c).wait_recv()
+            fixed[d] = s_v[d].astype(f32) + arr[ITERS - 1, d].astype(f32)
+            partials_wait(ITERS - 1, d)
+            assemble(ITERS - 1, d, out.at[d])
+
+        @pl.when(jnp.logical_not(takes(d)))
+        def _():
+            out[d] = s_v[d]
+
+        return carry
+
+    lax.fori_loop(0, 2, last, 0)
 
 
 def write_out(both, out_up, out_dn, sem):
@@ -393,6 +394,7 @@
             pltpu.VMEM((ITERS, 2, NX, k_own, cols), bf),
             pltpu.VMEM((ITERS, 2, NX, k_own, cols), bf),
             pltpu.VMEM((2, points, cols), bf),
+            pltpu.VMEM((2, points, cols), jnp.float32),
             sem((6,)),
             sem((2, CHUNKS)),
             sem((NX - 1,)),

time: 43.5 us -> 43.1 us (level)
  Pallas kernels: 42.8 us -> 42.3 us
    pallas_call x1, Pallas kernels: 41.7 us -> 41.3 us  [shards(): pl.pallas_call(kernel, out_shape=pltpu.VMEM((2, points, cols), bf), in_sp...]
where the time goes in v5:
time: 43.1 us; the launch traced here: 43 us
  Pallas kernels  42.3 us (98%)
  between operations  0.64 us (1%)
    pallas_call x1, Pallas kernels, shards(): pl.pallas_call(kernel, out_shape=pltpu.VMEM((2, points, cols), bf), in_sp...  41.3 us
    pallas_call x1, Pallas kernels, shards(): pl.pallas_call(write_out, out_shape=(jax.ShapeDtypeStruct(source_up.shape...  1.03 us

profile of v5, /device:TPU:9, one launch (start us, length us, event | category | flops | bytes accessed | tf_op | source)
XLA Modules:
  0.0 43.0 jit_solution(14844126126966998698)
XLA Ops:
  0.6 41.3 %traces.1.both = bf16[2,1024,256]{2,1,0:T(8,128)(2,1)S(1)} custom-call(bf16[1,1024,256]{2,1,0:T(8,128)(2,1)} %src_up.1, bf16[1,1024,256]{2,1,0:T(8,128)(2,1)} %src_dn.1, bf16[1,2,1024,1024]{3,2,1,0:T(8,128)(2,1)} %dg_up.1, bf16[1,2,1024,1024]{3,2,1,0:T(8,128)(2,1)} %dg_dn.1, bf16[1,2,32,1024]{3,2,1,0:T(8,128)(2,1)} %proj.1, bf16[1,2,32,1024]{3,2,1,0:T(8,128)(2,1)} %expn.1, ...), custom_call_target="tpu_custom_call" | custom-call | tf_op jit(solution)/shard_map/traces/pallas_call | solution.py:377
  41.9 1.0 %write_out.1 = (bf16[1,1024,256]{2,1,0:T(8,128)(2,1)}, bf16[1,1024,256]{2,1,0:T(8,128)(2,1)}) custom-call(bf16[2,1024,256]{2,1,0:T(8,128)(2,1)S(1)} %traces.1.both), custom_call_target="tpu_custom_call" | custom-call | tf_op jit(solution)/shard_map/write_out/pallas_call | solution.py:416

commit v6 on v5

--- a/solution.py
+++ b/solution.py
@@ -275,8 +275,8 @@
         advance(k, first)
         dense(k, first, 0, half)
         renew(k, second)
+        advance(k, second)
         dense(k, first, half, CHUNKS)
-        advance(k, second)
         dense(k, second, 0, CHUNKS)
 
         @pl.when(k == 0)

time: 43.1 us -> 43.1 us (level)
  no operation moved by 1% of the time
where the time goes in v6:
time: 43.1 us; the launch traced here: 43 us
  Pallas kernels  42.3 us (98%)
  between operations  0.64 us (1%)
    pallas_call x1, Pallas kernels, shards(): pl.pallas_call(kernel, out_shape=pltpu.VMEM((2, points, cols), bf), in_sp...  41.3 us
    pallas_call x1, Pallas kernels, shards(): pl.pallas_call(write_out, out_shape=(jax.ShapeDtypeStruct(source_up.shape...  1.03 us

profile of v6, /device:TPU:9, one launch (start us, length us, event | category | flops | bytes accessed | tf_op | source)
XLA Modules:
  0.0 43.0 jit_solution(6764751024928721786)
XLA Ops:
  0.6 41.3 %traces.1.both = bf16[2,1024,256]{2,1,0:T(8,128)(2,1)S(1)} custom-call(bf16[1,1024,256]{2,1,0:T(8,128)(2,1)} %src_up.1, bf16[1,1024,256]{2,1,0:T(8,128)(2,1)} %src_dn.1, bf16[1,2,1024,1024]{3,2,1,0:T(8,128)(2,1)} %dg_up.1, bf16[1,2,1024,1024]{3,2,1,0:T(8,128)(2,1)} %dg_dn.1, bf16[1,2,32,1024]{3,2,1,0:T(8,128)(2,1)} %proj.1, bf16[1,2,32,1024]{3,2,1,0:T(8,128)(2,1)} %expn.1, ...), custom_call_target="tpu_custom_call" | custom-call | tf_op jit(solution)/shard_map/traces/pallas_call | solution.py:377
  41.9 1.0 %write_out.1 = (bf16[1,1024,256]{2,1,0:T(8,128)(2,1)}, bf16[1,1024,256]{2,1,0:T(8,128)(2,1)}) custom-call(bf16[2,1024,256]{2,1,0:T(8,128)(2,1)S(1)} %traces.1.both), custom_call_target="tpu_custom_call" | custom-call | tf_op jit(solution)/shard_map/write_out/pallas_call | solution.py:416
